TPU v7x, 32 devices: a whole 2x2x4 slice. The times are simulated.
32 devices in a mesh: xy: 8 (over y, x, core), gz: 4 (over z).
Axes of the slice: x: 2, y: 2, z: 4, core: 2. Of those that a mesh axis runs over, the one named last changes fastest.
Arguments:
- features: bfloat16 [8, 2, 4, 64, 128], P('xy', None, 'gz'), may hold values from -6 to 6
- cotangent: bfloat16 [8, 2, 4, 64, 128], P('xy', None, 'gz'), may hold values from -6 to 6
- positions: float32 [8, 2, 4, 3, 64], P('xy', None, 'gz'), may hold values from 0 to 1
- counts: int32 [8, 2, 4], P('xy', None, 'gz'), may hold values from 32 to 64
- neighbour_mask: int32 [8, 2, 4, 27], P('xy', None, 'gz'), may hold values 0 or 1
- proj_weight: bfloat16 [128, 64], replicated, may hold values from -0.5 to 0.5
- out_weight: bfloat16 [64, 128], replicated, may hold values from -0.75 to 0.75
- radial_weight: float32 [8, 64], replicated, may hold values from -58 to 58
Outputs:
- updated: bfloat16 [8, 2, 4, 64, 128], P('xy', None, 'gz')
- feature_grad: bfloat16 [8, 2, 4, 64, 128], P('xy', None, 'gz')
Inputs may be any that keep to these rules, and one draw needn't show every extreme that they name: `counts`: the atoms of a cell beyond its count are padding.
All inputs are finite; a program needn't handle non-finite values. No bound on the sum of `neighbour_mask` on one device may be relied on, other than what follows from the above.
Results may differ from a plain program's by a relative error of at most 0.007.
Values may be sent and summed in bfloat16 or wider, within the bound.
A program may use at most 64 MiB of HBM per device.

v0:
```python
import functools

import jax
import jax.numpy as jnp
from jax import lax
from jax.experimental import pallas as pl
from jax.experimental.pallas import tpu as pltpu
from jax.sharding import PartitionSpec as P

MESH = pl.DeviceIdType.MESH
AXES = ("xy", "gz")
GROUPS = (((0, 0),), ((-1, 0), (1, 0)), ((0, -1), (-1, -1), (1, -1)), ((0, 1), (-1, 1), (1, 1)))
ORDER = ((-1, None), (1, None), (-1, True), (1, True), (-1, False), (1, False), (0, True), (0, False))
SLOT = {at: slot for slot, at in enumerate(at for group in GROUPS for at in group)}
F32 = jnp.float32
BF16 = jnp.bfloat16


def nt(a, b):
    return lax.dot_general(a, b, (((1,), (1,)), ((), ())), preferred_element_type=F32)


def tn(a, b):
    return lax.dot_general(a, b, (((0,), (0,)), ((), ())), preferred_element_type=F32)


def direction(ox, oy, oz):
    return (ox + 1) * 9 + (oy + 1) * 3 + oz + 1


def kernel(
    atoms,
    bases,
    feat_hbm,
    cot_hbm,
    pos_hbm,
    counts_hbm,
    mask_hbm,
    proj_hbm,
    outw_hbm,
    radial_hbm,
    both_ref,
    feat_ref,
    cot_ref,
    pos_ref,
    counts_ref,
    mask_ref,
    proj_ref,
    outw_ref,
    radial_ref,
    packet_out,
    packet_in,
    own_cols,
    tiles,
    source,
    grads,
    local_sem,
    send_sem,
    recv_sem,
):
    rows = feat_ref.shape[0]
    sizes = [lax.axis_size(axis) for axis in AXES]
    here = [lax.axis_index(axis) for axis in AXES]

    def device_at(ox, oz):
        return (lax.rem(here[0] + ox + sizes[0], sizes[0]), lax.rem(here[1] + oz + sizes[1], sizes[1]))

    sooner = jnp.where(here[1] == 0, 1, 0)
    later = 1 - sooner
    barrier = pltpu.get_barrier_semaphore()
    others = [(-1, 0), (1, 0), (-1, -1), (-1, 1), (1, -1), (1, 1), (0, -1), (0, 1)]
    for ox, oz in others[::-1]:
        pl.semaphore_signal(barrier, inc=1, device_id=device_at(ox, oz), device_id_type=MESH)

    fetches = [
        pltpu.make_async_copy(far, near, local_sem.at[at])
        for at, (far, near) in enumerate(
            (
                (mask_hbm, mask_ref),
                (counts_hbm, counts_ref),
                (pos_hbm, pos_ref),
                (proj_hbm, proj_ref),
                (feat_hbm, feat_ref),
                (radial_hbm, radial_ref),
                (outw_hbm, outw_ref),
                (cot_hbm, cot_ref),
            )
        )
    ]
    for fetch in fetches:
        fetch.start()
    for fetch in fetches[:3]:
        fetch.wait()

    lane = lax.broadcasted_iota(jnp.int32, (1, rows), 1)
    upper = lane >= atoms
    valid_lane = (lane - jnp.where(upper, atoms, 0)) < jnp.where(upper, counts_ref[1], counts_ref[0])
    valid_row = valid_lane.astype(F32)

    def lanes_of(slot):
        first = slot * rows
        return pl.ds(first if isinstance(slot, int) else pl.multiple_of(first, rows), rows)

    place = 2.0 * jnp.concatenate(
        [
            jnp.concatenate([pos_ref[axis], pos_ref[3 + axis]], axis=-1)
            for axis in range(3)
        ],
        axis=0,
    )
    for (ox, oz), slot in SLOT.items():
        listed = [
            jnp.where(
                upper,
                mask_ref[1, direction(ox, -oy, oz)].astype(F32),
                mask_ref[0, direction(ox, -oy, oz)].astype(F32),
            )
            for oy in (-1, 0, 1)
        ]
        packet = jnp.concatenate([place] + listed + [jnp.zeros((2, rows), F32)], axis=0)
        packet_out[slot] = packet
        if slot == 0:
            packet_in[0] = packet
    def held_at(kind, slot):
        if kind == 0:
            return packet_in.at[slot]
        return (source if kind == 1 else grads).at[:, lanes_of(slot)]

    def send(kind, src, slot, ox, oz):
        return pltpu.make_async_remote_copy(
            src_ref=src,
            dst_ref=held_at(kind, slot),
            send_sem=send_sem.at[kind, slot],
            recv_sem=recv_sem.at[kind, slot],
            device_id=device_at(ox, oz),
            device_id_type=MESH,
        )

    started = []

    def spread(kind):
        for ox, side in ORDER:
            if side is None:
                mine, theirs, oz = SLOT[ox, 0], SLOT[-ox, 0], 0
            else:
                which = later if side else sooner
                mine, theirs = SLOT[ox, -1] + 3 * which, SLOT[-ox, -1] + 3 * (1 - which)
                oz = 2 * which - 1
            src = packet_out.at[mine] if kind == 0 else held_at(kind, 0)
            copy = send(kind, src, theirs, ox, oz)
            copy.start()
            started.append(copy)

    def arrived(kind, slot):
        send(kind, held_at(kind, slot), slot, 1, 0).wait_recv()

    def build(ox, oz, slot):
        packet = packet_in[slot]
        other_x = packet[0:1] + 2.0 * ox
        other_y = packet[1:2]
        other_z = packet[2:3] + (2.0 * oz if isinstance(oz, int) else 2.0 * oz.astype(F32))
        middle_row = 4
        chunk = 32
        for c in range(2):
            cross = upper if c == 0 else jnp.logical_not(upper)
            low, same, high = (
                packet[middle_row + oy : middle_row + oy + 1]
                * mask_ref[c, direction(ox, oy, oz)].astype(F32)
                for oy in (-1, 0, 1)
            )
            gate_low = jnp.where(cross, low, same)
            gate_high = jnp.where(cross, high, same)
            move_low = jnp.where(cross, -2.0, 0.0)
            move_high = jnp.where(cross, 2.0, 0.0)

            def part(step, carry):
                first = pl.multiple_of(c * atoms + step * chunk, chunk)
                some = pl.ds(first, chunk)
                dx = other_x - own_cols[0, some, :]
                dy = other_y - own_cols[1, some, :]
                dz = other_z - own_cols[2, some, :]
                above = dy > 0.0
                dy = dy + jnp.where(above, move_low, move_high)
                gate = jnp.where(above, gate_low, gate_high)
                near = jnp.minimum(dx * dx + dy * dy + dz * dz, 1.0)
                room = 1.0 - near
                envelope = room * room * gate
                if isinstance(slot, int) and slot == 0:
                    at_row = lax.broadcasted_iota(jnp.int32, (chunk, rows), 0) + first
                    at_lane = lax.broadcasted_iota(jnp.int32, (chunk, rows), 1)
                    envelope = jnp.where(at_row == at_lane, 0.0, envelope)
                half = bases // 2
                v = bases * near - half
                up = jnp.exp(2.0 * v)
                down = jnp.exp(-2.0 * v)
                middle = envelope * jnp.exp(-2.0 * (v * v) - 0.5)
                up2, down2 = up * up, down * down
                high_value, low_value = middle * up, middle * down
                for step_out in range(half):
                    if step_out:
                        fall = EXP_FALL[step_out]
                        high_value = high_value * (up2 * fall)
                        low_value = low_value * (down2 * fall)
                    for b, value in ((half + step_out, high_value), (half - 1 - step_out, low_value)):
                        tiles[b, some, lanes_of(slot)] = value.astype(BF16)
                return carry

            lax.fori_loop(0, atoms // chunk, part, 0)

    def gathered(held, slot, count, total):
        width = count * rows
        first = slot * rows
        span = pl.ds(first if isinstance(slot, int) else pl.multiple_of(first, rows), width)
        stack = tiles[:, :, span].reshape(bases * rows, width)
        sums = nt(stack, held[:, span])
        for b in range(bases):
            term = sums[b * rows : (b + 1) * rows] * radial_ref[b : b + 1, :]
            total = term if total is None else total + term
        return total

    pl.semaphore_wait(barrier, len(others))
    spread(0)
    for fetch in fetches[3:5]:
        fetch.wait()
    projected = nt(proj_ref[...], feat_ref[...])
    source[:, lanes_of(0)] = (projected * valid_row).astype(BF16)
    spread(1)
    columns = jnp.concatenate([place, jnp.zeros((5, rows), F32)], axis=0).T
    for axis in range(3):
        own_cols[axis] = jnp.broadcast_to(columns[:, axis : axis + 1], (rows, rows))


    for fetch in fetches[5:]:
        fetch.wait()
    build(0, 0, 0)
    message = gathered(source, 0, 1, None)
    grad_act = nt(outw_ref[...], cot_ref[...])
    for at in GROUPS[1]:
        arrived(0, SLOT[at])
        build(*at, SLOT[at])
    for at in GROUPS[1]:
        arrived(1, SLOT[at])
    message = gathered(source, 1, 2, message)
    for which, oz in ((sooner, 2 * sooner - 1), (later, 2 * later - 1)):
        for at, ox in enumerate((0, -1, 1)):
            arrived(0, 3 + 3 * which + at)
            build(ox, oz, 3 + 3 * which + at)
        for at in range(3):
            arrived(1, 3 + 3 * which + at)
        message = gathered(source, 3 + 3 * which, 3, message)

    message = message.T * valid_row
    gate = 1.0 / (1.0 + jnp.exp(-message))
    grad_msg = grad_act * gate * (1.0 + message * (1.0 - gate)) * valid_row
    grads[:, lanes_of(0)] = grad_msg.astype(BF16)
    spread(2)

    activated = (message * gate).astype(BF16)
    both_ref[0] = (feat_ref[...].astype(F32) + tn(activated, outw_ref[...])).astype(BF16)

    total = gathered(grads, 0, 1, None)
    for at in (1, 2):
        arrived(2, at)
    total = gathered(grads, 1, 2, total)
    for which in (sooner, later):
        for at in range(3):
            arrived(2, 3 + 3 * which + at)
        total = gathered(grads, 3 + 3 * which, 3, total)
    at_row = lax.broadcasted_iota(jnp.int32, total.shape, 0)
    in_upper = at_row >= atoms
    kept = (at_row - jnp.where(in_upper, atoms, 0)) < jnp.where(in_upper, counts_ref[1], counts_ref[0])
    grad_proj = jnp.where(kept, total, 0.0).astype(BF16)
    pulled = jnp.dot(grad_proj, proj_ref[...], preferred_element_type=F32)
    both_ref[1] = (cot_ref[...].astype(F32) + pulled).astype(BF16)

    for copy in started:
        copy.wait_send()


EXP_FALL = [2.718281828459045 ** (-4.0 * step) for step in range(8)]


def on_device(
    features, cotangent, positions, counts, neighbour_mask, proj_weight, out_weight, radial_weight
):
    shape = features.shape
    cells, atoms, channels = shape[1], shape[3], shape[4]
    bases, width = radial_weight.shape
    rows = cells * atoms
    assert shape[0] == 1 and shape[2] == 1 and cells == 2
    operands = (
        features.reshape(rows, channels),
        cotangent.reshape(rows, channels),
        positions.reshape(cells * 3, 1, atoms),
        counts.reshape(cells),
        neighbour_mask.reshape(cells, neighbour_mask.shape[-1]),
        proj_weight.T,
        out_weight,
        radial_weight,
    )
    held = [pltpu.SMEM if at in (3, 4) else pltpu.VMEM for at in range(len(operands))]
    both = pl.pallas_call(
        functools.partial(kernel, atoms, bases),
        out_shape=pltpu.VMEM((2, rows, channels), BF16),
        in_specs=[pl.BlockSpec(memory_space=pl.ANY)] * len(operands),
        out_specs=pl.BlockSpec(memory_space=pltpu.VMEM),
        scratch_shapes=[space(x.shape, x.dtype) for space, x in zip(held, operands)]
        + [
            pltpu.VMEM((9, 8, rows), F32),
            pltpu.VMEM((9, 8, rows), F32),
            pltpu.VMEM((3, rows, rows), F32),
            pltpu.VMEM((bases, rows, 9 * rows), BF16),
            pltpu.VMEM((width, 9 * rows), BF16),
            pltpu.VMEM((width, 9 * rows), BF16),
            pltpu.SemaphoreType.DMA((10,)),
            pltpu.SemaphoreType.DMA((3, 9)),
            pltpu.SemaphoreType.DMA((3, 9)),
        ],
        compiler_params=pltpu.CompilerParams(collective_id=0, has_side_effects=True),
    )(*operands)
    return both[0].reshape(shape), both[1].reshape(shape)


def solution(mesh):
    cell = P("xy", None, "gz", None, None)
    return jax.shard_map(
        on_device,
        mesh=mesh,
        in_specs=(cell, cell, cell, P("xy", None, "gz"), P("xy", None, "gz", None), P(), P(), P()),
        out_specs=(cell, cell),
        check_vma=False,
    )
```

profile of v0, /device:TPU:0, one launch (start us, length us, event | category | flops | bytes accessed | tf_op | source)
XLA Modules:
  0.0 18.7 jit_solution(9705127746524109847)
XLA Ops:
  0.6 17.4 %shard_map.95 = bf16[2,128,128]{2,1,0:T(8,128)(2,1)S(1)} custom-call(bf16[128,128]{1,0:T(8,128)(2,1)} %bitcast.12, bf16[128,128]{1,0:T(8,128)(2,1)} %bitcast.13, f32[6,1,64]{2,1,0:T(1,128)} %bitcast.17, s32[2]{0:T(128)} %bitcast.19, s32[2,27]{1,0:T(2,128)} %bitcast.18, bf16[64,128]{1,0:T(8,128)(2,1)} %bitcast.16, bf16[64,128]{1,0:T(8,128)(2,1)} %outw_hbm.1, ...), custom_call_target="tpu_custom_call" | custom-call | tf_op jit(solution)/shard_map/pallas_call | solution.py:302
  18.0 0.6 %fusion = (bf16[1,128,128]{2,1,0:T(8,128)(2,1)}, bf16[1,128,128]{2,1,0:T(8,128)(2,1)}) fusion(bf16[2,128,128]{2,1,0:T(8,128)(2,1)S(1)} %shard_map.95), kind=kLoop, calls=%fused_computation | loop fusion | bytes 131072 | tf_op jit(solution)/shard_map/slice | solution.py:321
where the time goes:
time: 18.8 us; the launch traced here: 18.7 us
  Pallas kernels  17.4 us (93%)
  between operations  0.64 us (3%)
  local copies, waits for them, and re-layouts  0.63 us (3%)
    pallas_call x1, Pallas kernels, on_device(): pl.pallas_call(functools.partial(kernel, atoms, bases), out_shape=pltpu.V...  17.4 us
    slice x1, local copies, waits for them, and re-layouts, on_device(): return (both[0].reshape(shape), both[1].reshape(shape))  0.63 us

commit v1 on v0

v1 whole, which is shorter than its diff:
```python
import functools

import jax
import jax.numpy as jnp
from jax import lax
from jax.experimental import pallas as pl
from jax.experimental.pallas import tpu as pltpu
from jax.sharding import PartitionSpec as P

MESH = pl.DeviceIdType.MESH
AXES = ("xy", "gz")
F32 = jnp.float32
BF16 = jnp.bfloat16
LOG2E = 1.4426950408889634

SAME, INNER, OUTER = 0, 1, 2
LEVEL, SOONER, LATER = 0, 1, 2
SLOTS = {1: (INNER, LEVEL), 2: (OUTER, LEVEL)}
SLOTS.update({3 + at: (at, SOONER) for at in (SAME, INNER, OUTER)})
SLOTS.update({6 + at: (at, LATER) for at in (SAME, INNER, OUTER)})
GROUPS = ((0, 1), (2, 3), (4, 5), (6, 7), (8,))
WAITS = {(0, 1): (1, 2), (2, 3): (3,), (4, 5): (4, 5), (6, 7): (6, 7), (8,): (8,)}


def nt(a, b):
    return lax.dot_general(a, b, (((1,), (1,)), ((), ())), preferred_element_type=F32)


def tn(a, b):
    return lax.dot_general(a, b, (((0,), (0,)), ((), ())), preferred_element_type=F32)


def direction(ox, oy, oz):
    return (ox + 1) * 9 + (oy + 1) * 3 + oz + 1


def basis_scale(bases):
    off = lax.broadcasted_iota(jnp.int32, (bases, 1), 0).astype(F32) - 0.5 * (bases - 1)
    return jnp.exp(-2.0 * off * off)


def kernel(
    atoms,
    bases,
    feat_hbm,
    cot_hbm,
    pos_hbm,
    counts_hbm,
    mask_hbm,
    proj_hbm,
    outw_hbm,
    radial_hbm,
    both_ref,
    feat_ref,
    cot_ref,
    pos_ref,
    counts_ref,
    mask_ref,
    proj_ref,
    outw_ref,
    radial_ref,
    packet_out,
    packet_in,
    relay,
    own_cols,
    tiles,
    weights,
    source,
    grads,
    local_sem,
    relay_sem,
    told_sem,
    send_sem,
    recv_sem,
):
    rows = feat_ref.shape[0]
    size_x, size_z = [lax.axis_size(axis) for axis in AXES]
    assert size_x % 2 == 0 and size_z >= 4
    here_x, here_z = [lax.axis_index(axis) for axis in AXES]
    first_z, second_z, last_z = here_z == 0, here_z == 1, here_z == size_z - 1

    odd_x = lax.rem(here_x, 2) == 1
    inward = jnp.where(odd_x, -1, 1)
    off_x = (0, inward, -inward)
    near_z = jnp.where(first_z, 1, -1)
    off_z = (0, near_z, -near_z)
    at_x = [here_x] + [lax.rem(here_x + off + size_x, size_x) for off in off_x[1:]]
    at_z = [here_z] + [lax.rem(here_z + off + size_z, size_z) for off in off_z[1:]]

    into_z = [0] + [
        jnp.where(jnp.where(at_z[side] == 0, 1, -1) == -off_z[side], 3, 6) for side in (SOONER, LATER)
    ]

    def slot_there(slot):
        column, level = SLOTS[slot]
        return slot if level == LEVEL else into_z[level] + column

    def device(slot):
        column, level = SLOTS[slot]
        return (at_x[column], at_z[level])

    barrier = pltpu.get_barrier_semaphore()

    def greet(column, z):
        pl.semaphore_signal(barrier, inc=1, device_id=(at_x[column], z), device_id_type=MESH)

    later_z = jnp.where(last_z, 1, at_z[LATER])
    for column in (OUTER, SAME, INNER):
        greet(column, later_z)
    greet(SAME, at_z[SOONER])

    @pl.when(jnp.logical_not(second_z))
    def _():
        greet(OUTER, at_z[SOONER])
        greet(INNER, at_z[SOONER])

    @pl.when(jnp.logical_not(jnp.logical_and(first_z, odd_x)))
    def _():
        greet(OUTER, here_z)
        greet(INNER, here_z)

    fetches = [
        pltpu.make_async_copy(far, near, local_sem.at[at])
        for at, far, near in (
            (0, mask_hbm, mask_ref),
            (1, counts_hbm, counts_ref),
            (2, pos_hbm, pos_ref),
            (3, proj_hbm, proj_ref),
            (3, feat_hbm, feat_ref),
            (4, radial_hbm, radial_ref),
            (5, outw_hbm, outw_ref),
            (5, cot_hbm, cot_ref),
        )
    ]
    for fetch in fetches:
        fetch.start()

    def fetched_pair(at):
        both = source.at[0 : 1 + rows // proj_ref.shape[0]]
        pltpu.make_async_copy(both, both, local_sem.at[at]).wait()

    with jax.named_scope("fetch"):
        for fetch in fetches[:3]:
            fetch.wait()

    lane = lax.broadcasted_iota(jnp.int32, (1, rows), 1)
    upper = lane >= atoms
    valid_lane = (lane - jnp.where(upper, atoms, 0)) < jnp.where(upper, counts_ref[1], counts_ref[0])
    valid_row = valid_lane.astype(F32)

    place = 2.0 * jnp.concatenate(
        [jnp.concatenate([pos_ref[axis], pos_ref[3 + axis]], axis=-1) for axis in range(3)], axis=0
    )

    def packet_for(ox, oz):
        listed = [
            jnp.where(
                upper,
                mask_ref[1, direction(ox, -oy, oz)].astype(F32),
                mask_ref[0, direction(ox, -oy, oz)].astype(F32),
            )
            for oy in (-1, 0, 1)
        ]
        return jnp.concatenate([place] + listed + [jnp.zeros((2, rows), F32)], axis=0)

    packet_in[0] = packet_for(0, 0)
    for slot, (column, level) in SLOTS.items():
        packet_out[slot] = packet_for(off_x[column], off_z[level])

    def held_at(kind, slot):
        return (packet_in, source, grads)[kind].at[slot]

    def remote(src, dst, send, recv, to):
        return pltpu.make_async_remote_copy(
            src_ref=src,
            dst_ref=dst,
            send_sem=send,
            recv_sem=recv,
            device_id=to,
            device_id_type=MESH,
        )

    def lands(kind, slot):
        if kind == 0:
            return slot - 1
        return 5 * kind + (3, 3, 4, 5, 5, 6, 6, 7)[slot - 1]

    def landing(kind, slot):
        level = SLOTS[slot][1]
        if level == LEVEL:
            return recv_sem.at[lands(kind, slot)]
        column = SLOTS[slot][0]
        return recv_sem.at[jnp.where(into_z[level] == 3, lands(kind, 3 + column), lands(kind, 6 + column))]

    def spread(kind, slots):
        for slot in slots:
            column, level = SLOTS[slot]
            src = packet_out.at[slot] if kind == 0 else held_at(kind, 0)
            there = slot_there(slot)
            remote(src, held_at(kind, there), send_sem.at[kind], landing(kind, slot), device(slot)).start()

    def arrived(kind, low, high):
        held = (packet_in, source, grads)[kind].at[low:high]
        remote(held, held, send_sem.at[kind], recv_sem.at[lands(kind, low)], device(1)).wait_recv()

    def sent(kind, count):
        some = (packet_in, source, grads)[kind].at[0:count]
        remote(some, some, send_sem.at[kind], recv_sem.at[0], device(1)).wait_send()

    def build(slot):
        column, level = SLOTS[slot] if slot else (SAME, LEVEL)
        ox, oz = off_x[column], off_z[level]
        packet = packet_in[slot]
        other_x = packet[0:1] + 2.0 * (ox if column == SAME else ox.astype(F32))
        other_y = packet[1:2]
        other_z = packet[2:3] + 2.0 * (oz if level == LEVEL else oz.astype(F32))
        middle_row = 4
        chunk = 32
        for c in range(2):
            cross = upper if c == 0 else jnp.logical_not(upper)
            low, same, high = (
                packet[middle_row + oy : middle_row + oy + 1]
                * mask_ref[c, direction(ox, oy, oz)].astype(F32)
                for oy in (-1, 0, 1)
            )
            gate_low = jnp.where(cross, low, same)
            gate_high = jnp.where(cross, high, same)
            move = jnp.where(cross, 2.0, 0.0)

            for first in range(c * atoms, (c + 1) * atoms, chunk):
                some = pl.ds(first, chunk)
                dx = other_x - own_cols[0, some, :]
                dy = other_y - own_cols[1, some, :]
                dz = other_z - own_cols[2, some, :]
                gate = jnp.where(dy > 0.0, gate_low, gate_high)
                dy = jnp.abs(dy) - move
                near = jnp.minimum(dx * dx + dy * dy + dz * dz, 1.0)
                room = 1.0 - near
                envelope = room * room * gate
                if slot == 0:
                    at_row = lax.broadcasted_iota(jnp.int32, (chunk, rows), 0) + first
                    at_lane = lax.broadcasted_iota(jnp.int32, (chunk, rows), 1)
                    envelope = jnp.where(at_row == at_lane, 0.0, envelope)
                half = bases // 2
                rise = (4.0 * LOG2E) * (bases * near - half)
                up, down = jnp.exp2(rise), jnp.exp2(-rise)
                high = envelope * jnp.exp2(rise * (0.5 - rise * (0.125 / LOG2E)))
                low = high * down
                for step_out in range(half):
                    if step_out:
                        high, low = high * up, low * down
                    for b, value in ((half + step_out, high), (half - 1 - step_out, low)):
                        tiles[slot * bases + b, some, :] = value.astype(BF16)

    def gathered(held, slots, total):
        values = jnp.concatenate([held[slot] for slot in slots], axis=1)
        built = [tiles[slot * bases : (slot + 1) * bases].reshape(bases * rows, rows) for slot in slots]
        sums = nt(values, jnp.concatenate(built, axis=1))
        for b in range(bases):
            term = sums[:, b * rows : (b + 1) * rows] * weights[b]
            total = term if total is None else total + term
        return total

    fetched_pair(3)
    projected = nt(proj_ref[...], feat_ref[...])
    source[0] = (projected * valid_row).astype(BF16)

    heard = jnp.where(first_z, jnp.where(odd_x, 3, 1), jnp.where(second_z, 11, 8))

    @pl.when(here_z > 1)
    def _():
        with jax.named_scope("barrier"):
            pl.semaphore_wait(barrier, heard)
        spread(0, (2, 1, 8, 6, 7, 3, 5, 4))
        spread(1, (2, 1, 8, 6, 7, 3, 5, 4))

    with jax.named_scope("own"):
        columns = jnp.concatenate([place, jnp.zeros((5, rows), F32)], axis=0).T
        for axis in range(3):
            own_cols[axis] = jnp.broadcast_to(columns[:, axis : axis + 1], (rows, rows))
        fetches[5].wait()
        radial = (radial_ref[...] * basis_scale(bases)).T
        for b in range(bases):
            weights[b] = jnp.broadcast_to(radial[:, b : b + 1], (radial.shape[0], rows))
        fetched_pair(5)
        build(0)
        grad_act = nt(outw_ref[...], cot_ref[...])

    with jax.named_scope("spread"):

        @pl.when(first_z)
        def _():
            with jax.named_scope("barrier"):
                pl.semaphore_wait(barrier, heard)
            spread(1, (3,))
            remote(packet_out.at[6:9], relay, send_sem.at[0], relay_sem, device(3)).start()
            spread(0, (3,))

            @pl.when(odd_x)
            def _():
                for slot in (2, 1):
                    pl.semaphore_signal(told_sem.at[0], inc=1, device_id=device(slot), device_id_type=MESH)

            @pl.when(jnp.logical_not(odd_x))
            def _():
                pl.semaphore_wait(told_sem.at[0], 2)

            spread(0, (2, 1))
            spread(1, (2, 1))
            with jax.named_scope("told"):
                pl.semaphore_wait(told_sem.at[1], 1)
            spread(0, (5, 4))
            spread(1, (5, 4))

        @pl.when(second_z)
        def _():
            with jax.named_scope("barrier"):
                pl.semaphore_wait(barrier, heard)
            pl.semaphore_signal(told_sem.at[1], inc=1, device_id=device(3), device_id_type=MESH)
            spread(0, (2, 1, 3, 5, 4))
            spread(1, (2, 1, 3, 5, 4))
            with jax.named_scope("relay"):
                arrived(1, 3, 4)
                remote(relay, relay, send_sem.at[0], relay_sem, device(1)).wait_recv()
            for column in (OUTER, SAME, INNER):
                to = (at_x[column], size_z - 1)
                there = 6 + column
                for kind, src in ((0, relay.at[column]), (1, held_at(1, 3))):
                    land = recv_sem.at[lands(kind, there)]
                    remote(src, held_at(kind, there), send_sem.at[kind], land, to).start()
            spread(0, (8, 6, 7))
            spread(1, (8, 6, 7))

    def take(kind, slot):
        if kind == 0:
            arrived(0, slot, slot + 1)
        elif kind == 1 and slot == 3:
            pl.when(jnp.logical_not(second_z))(lambda: arrived(1, 3, 4))
        elif slot == 8 or lands(kind, slot + 1) != lands(kind, slot):
            low = min(at for at in range(1, 9) if lands(kind, at) == lands(kind, slot))
            arrived(kind, low, slot + 1)

    message = None
    for group in GROUPS:
        for slot in group:
            if slot:
                with jax.named_scope(f"p{slot}"):
                    take(0, slot)
                with jax.named_scope("build"):
                    build(slot)
        with jax.named_scope(f"s{group[-1]}"):
            for slot in WAITS[group]:
                take(1, slot)
        with jax.named_scope("gather"):
            message = gathered(source, group, message)

    message = message * valid_row
    gate = 1.0 / (1.0 + jnp.exp(-message))
    grad_msg = grad_act * gate * (1.0 + message * (1.0 - gate)) * valid_row
    grads[0] = grad_msg.astype(BF16)
    with jax.named_scope("spread2"):
        spread(2, (8, 6, 7, 3, 5, 4, 2, 1))

    activated = (message * gate).astype(BF16)
    both_ref[0] = (feat_ref[...].astype(F32) + tn(activated, outw_ref[...])).astype(BF16)

    total = None
    for group in GROUPS:
        with jax.named_scope(f"g{group[-1]}"):
            for slot in WAITS[group]:
                take(2, slot)
        with jax.named_scope("gather2"):
            total = gathered(grads, group, total)
    grad_proj = (total * valid_row).astype(BF16)
    pulled = tn(grad_proj, proj_ref[...])
    both_ref[1] = (cot_ref[...].astype(F32) + pulled).astype(BF16)

    with jax.named_scope("sent"):
        sent(0, 8)
        sent(1, 5)
        sent(2, 8)

        @pl.when(jnp.logical_not(first_z))
        def _():
            sent(1, 3)

        @pl.when(second_z)
        def _():
            sent(0, 3)
            sent(1, 3)


def on_device(
    features, cotangent, positions, counts, neighbour_mask, proj_weight, out_weight, radial_weight
):
    shape = features.shape
    cells, atoms, channels = shape[1], shape[3], shape[4]
    bases, width = radial_weight.shape
    rows = cells * atoms
    assert shape[0] == 1 and shape[2] == 1 and cells == 2
    operands = (
        features.reshape(rows, channels),
        cotangent.reshape(rows, channels),
        positions.reshape(cells * 3, 1, atoms),
        counts.reshape(cells),
        neighbour_mask.reshape(cells, neighbour_mask.shape[-1]),
        proj_weight.T,
        out_weight,
        radial_weight,
    )
    held = [pltpu.SMEM if at in (3, 4) else pltpu.VMEM for at in range(len(operands))]
    both = pl.pallas_call(
        functools.partial(kernel, atoms, bases),
        out_shape=pltpu.VMEM((2, rows, channels), BF16),
        in_specs=[pl.BlockSpec(memory_space=pl.ANY)] * len(operands),
        out_specs=pl.BlockSpec(memory_space=pltpu.VMEM),
        scratch_shapes=[space(x.shape, x.dtype) for space, x in zip(held, operands)]
        + [
            pltpu.VMEM((9, 8, rows), F32),
            pltpu.VMEM((9, 8, rows), F32),
            pltpu.VMEM((3, 8, rows), F32),
            pltpu.VMEM((3, rows, rows), F32),
            pltpu.VMEM((9 * bases, rows, rows), BF16),
            pltpu.VMEM((bases, width, rows), F32),
            pltpu.VMEM((9, width, rows), BF16),
            pltpu.VMEM((9, width, rows), BF16),
            pltpu.SemaphoreType.DMA((6,)),
            pltpu.SemaphoreType.DMA,
            pltpu.SemaphoreType.REGULAR((2,)),
            pltpu.SemaphoreType.DMA((3,)),
            pltpu.SemaphoreType.DMA((18,)),
        ],
        compiler_params=pltpu.CompilerParams(collective_id=0, has_side_effects=True),
    )(*operands)
    return both[0].reshape(shape), both[1].reshape(shape)


def solution(mesh):
    cell = P("xy", None, "gz", None, None)
    return jax.shard_map(
        on_device,
        mesh=mesh,
        in_specs=(cell, cell, cell, P("xy", None, "gz"), P("xy", None, "gz", None), P(), P(), P()),
        out_specs=(cell, cell),
        check_vma=False,
    )
```

time: 18.8 us -> 17.8 us (0.947)
  Pallas kernels: 17.4 us -> 16.3 us
    pallas_call x1, Pallas kernels: 17.4 us -> 16.3 us  [on_device(): pl.pallas_call(functools.partial(kernel, atoms, bases), out_shape=pltpu.V...]
where the time goes in v1:
time: 17.8 us; the launch traced here: 17.5 us
  Pallas kernels  16.3 us (92%)
  between operations  0.64 us (4%)
  local copies, waits for them, and re-layouts  0.63 us (4%)
    pallas_call x1, Pallas kernels, on_device(): pl.pallas_call(functools.partial(kernel, atoms, bases), out_shape=pltpu.V...  16.3 us
    slice x1, local copies, waits for them, and re-layouts, on_device(): return (both[0].reshape(shape), both[1].reshape(shape))  0.63 us

profile of v1, /device:TPU:0, one launch (start us, length us, event | category | flops | bytes accessed | tf_op | source)
XLA Modules:
  0.0 17.5 jit_solution(8303789114712426284)
XLA Ops:
  0.6 16.3 %shard_map.95 = bf16[2,128,128]{2,1,0:T(8,128)(2,1)S(1)} custom-call(bf16[128,128]{1,0:T(8,128)(2,1)} %bitcast.12, bf16[128,128]{1,0:T(8,128)(2,1)} %bitcast.13, f32[6,1,64]{2,1,0:T(1,128)} %bitcast.17, s32[2]{0:T(128)} %bitcast.19, s32[2,27]{1,0:T(2,128)} %bitcast.18, bf16[64,128]{1,0:T(8,128)(2,1)} %bitcast.16, bf16[64,128]{1,0:T(8,128)(2,1)} %outw_hbm.1, ...), custom_call_target="tpu_custom_call" | custom-call | tf_op jit(solution)/shard_map/pallas_call | solution.py:412
  16.9 0.6 %fusion = (bf16[1,128,128]{2,1,0:T(8,128)(2,1)}, bf16[1,128,128]{2,1,0:T(8,128)(2,1)}) fusion(bf16[2,128,128]{2,1,0:T(8,128)(2,1)S(1)} %shard_map.95), kind=kLoop, calls=%fused_computation | loop fusion | bytes 131072 | tf_op jit(solution)/shard_map/slice | solution.py:435

commit v2 on v1

--- a/solution.py
+++ b/solution.py
@@ -12,14 +12,23 @@
 F32 = jnp.float32
 BF16 = jnp.bfloat16
 LOG2E = 1.4426950408889634
+PIECES = 4
 
 SAME, INNER, OUTER = 0, 1, 2
 LEVEL, SOONER, LATER = 0, 1, 2
 SLOTS = {1: (INNER, LEVEL), 2: (OUTER, LEVEL)}
 SLOTS.update({3 + at: (at, SOONER) for at in (SAME, INNER, OUTER)})
 SLOTS.update({6 + at: (at, LATER) for at in (SAME, INNER, OUTER)})
-GROUPS = ((0, 1), (2, 3), (4, 5), (6, 7), (8,))
-WAITS = {(0, 1): (1, 2), (2, 3): (3,), (4, 5): (4, 5), (6, 7): (6, 7), (8,): (8,)}
+STAGES = (
+    ((1,), (), ()),
+    ((2, 6), (1,), (0, 1)),
+    ((7, 8), (2, 6), (2, 6)),
+    ((), (7, 8), (7, 8)),
+    ((3,), (), ()),
+    ((5,), (), ()),
+    ((4,), (3, 5), (3, 5)),
+    ((), (4,), (4,)),
+)
 
 
 def nt(a, b):
@@ -67,6 +76,7 @@
     weights,
     source,
     grads,
+    owes,
     local_sem,
     relay_sem,
     told_sem,
@@ -82,13 +92,16 @@
     odd_x = lax.rem(here_x, 2) == 1
     inward = jnp.where(odd_x, -1, 1)
     off_x = (0, inward, -inward)
-    near_z = jnp.where(first_z, 1, -1)
-    off_z = (0, near_z, -near_z)
+
+    def sooner_of(z):
+        return jnp.where(jnp.logical_or(z == 0, z == size_z - 1), 1, -1)
+
+    off_z = (0, sooner_of(here_z), -sooner_of(here_z))
     at_x = [here_x] + [lax.rem(here_x + off + size_x, size_x) for off in off_x[1:]]
     at_z = [here_z] + [lax.rem(here_z + off + size_z, size_z) for off in off_z[1:]]
 
     into_z = [0] + [
-        jnp.where(jnp.where(at_z[side] == 0, 1, -1) == -off_z[side], 3, 6) for side in (SOONER, LATER)
+        jnp.where(sooner_of(at_z[side]) == -off_z[side], 3, 6) for side in (SOONER, LATER)
     ]
 
     def slot_there(slot):
@@ -104,15 +117,16 @@
     def greet(column, z):
         pl.semaphore_signal(barrier, inc=1, device_id=(at_x[column], z), device_id_type=MESH)
 
-    later_z = jnp.where(last_z, 1, at_z[LATER])
-    for column in (OUTER, SAME, INNER):
-        greet(column, later_z)
-    greet(SAME, at_z[SOONER])
+    sooner_z = jnp.where(last_z, 1, at_z[SOONER])
 
     @pl.when(jnp.logical_not(second_z))
     def _():
-        greet(OUTER, at_z[SOONER])
-        greet(INNER, at_z[SOONER])
+        greet(OUTER, sooner_z)
+        greet(INNER, sooner_z)
+
+    greet(SAME, sooner_z)
+    for column in (OUTER, SAME, INNER):
+        greet(column, at_z[LATER])
 
     @pl.when(jnp.logical_not(jnp.logical_and(first_z, odd_x)))
     def _():
@@ -183,7 +197,7 @@
     def lands(kind, slot):
         if kind == 0:
             return slot - 1
-        return 5 * kind + (3, 3, 4, 5, 5, 6, 6, 7)[slot - 1]
+        return 8 + (0, 1, 2, 3, 4, 5, 6, 6)[slot - 1]
 
     def landing(kind, slot):
         level = SLOTS[slot][1]
@@ -214,52 +228,72 @@
         other_x = packet[0:1] + 2.0 * (ox if column == SAME else ox.astype(F32))
         other_y = packet[1:2]
         other_z = packet[2:3] + 2.0 * (oz if level == LEVEL else oz.astype(F32))
-        middle_row = 4
         chunk = 32
+        half = bases // 2
+
+        def step(first, gate_low, gate_high, move):
+            some = slice(first, first + chunk)
+            dx = other_x - own_cols[0, some, :]
+            dy = other_y - own_cols[1, some, :]
+            dz = other_z - own_cols[2, some, :]
+            gate = jnp.where(dy > 0.0, gate_low, gate_high)
+            dy = jnp.abs(dy) - move
+            near = jnp.minimum(dx * dx + dy * dy + dz * dz, 1.0)
+            room = 1.0 - near
+            envelope = room * room * gate
+            if slot == 0:
+                at_row = lax.broadcasted_iota(jnp.int32, (chunk, rows), 0) + first
+                at_lane = lax.broadcasted_iota(jnp.int32, (chunk, rows), 1)
+                envelope = jnp.where(at_row == at_lane, 0.0, envelope)
+            rise = (4.0 * LOG2E * bases) * near - (4.0 * LOG2E * half)
+            up, down = jnp.exp2(rise), jnp.exp2(-rise)
+            high = envelope * jnp.exp2(rise * (0.5 - rise * (0.125 / LOG2E)))
+            low = high * down
+            for step_out in range(half):
+                if step_out:
+                    high, low = high * up, low * down
+                for b, value in ((half + step_out, high), (half - 1 - step_out, low)):
+                    tiles[slot * bases + b, some, :] = value.astype(BF16)
+
         for c in range(2):
             cross = upper if c == 0 else jnp.logical_not(upper)
             low, same, high = (
-                packet[middle_row + oy : middle_row + oy + 1]
-                * mask_ref[c, direction(ox, oy, oz)].astype(F32)
-                for oy in (-1, 0, 1)
+                packet[4 + oy : 5 + oy] * mask_ref[c, direction(ox, oy, oz)].astype(F32) for oy in (-1, 0, 1)
             )
             gate_low = jnp.where(cross, low, same)
             gate_high = jnp.where(cross, high, same)
             move = jnp.where(cross, 2.0, 0.0)
-
             for first in range(c * atoms, (c + 1) * atoms, chunk):
-                some = pl.ds(first, chunk)
-                dx = other_x - own_cols[0, some, :]
-                dy = other_y - own_cols[1, some, :]
-                dz = other_z - own_cols[2, some, :]
-                gate = jnp.where(dy > 0.0, gate_low, gate_high)
-                dy = jnp.abs(dy) - move
-                near = jnp.minimum(dx * dx + dy * dy + dz * dz, 1.0)
-                room = 1.0 - near
-                envelope = room * room * gate
-                if slot == 0:
-                    at_row = lax.broadcasted_iota(jnp.int32, (chunk, rows), 0) + first
-                    at_lane = lax.broadcasted_iota(jnp.int32, (chunk, rows), 1)
-                    envelope = jnp.where(at_row == at_lane, 0.0, envelope)
-                half = bases // 2
-                rise = (4.0 * LOG2E) * (bases * near - half)
-                up, down = jnp.exp2(rise), jnp.exp2(-rise)
-                high = envelope * jnp.exp2(rise * (0.5 - rise * (0.125 / LOG2E)))
-                low = high * down
-                for step_out in range(half):
-                    if step_out:
-                        high, low = high * up, low * down
-                    for b, value in ((half + step_out, high), (half - 1 - step_out, low)):
-                        tiles[slot * bases + b, some, :] = value.astype(BF16)
-
-    def gathered(held, slots, total):
-        values = jnp.concatenate([held[slot] for slot in slots], axis=1)
-        built = [tiles[slot * bases : (slot + 1) * bases].reshape(bases * rows, rows) for slot in slots]
-        sums = nt(values, jnp.concatenate(built, axis=1))
-        for b in range(bases):
-            term = sums[:, b * rows : (b + 1) * rows] * weights[b]
-            total = term if total is None else total + term
+                yield functools.partial(step, first, gate_low, gate_high, move)
+
+    def gathered(slots, total, building=()):
+        steps = [step for slot in building for step in build(slot)]
+        values = jnp.concatenate([source[slot] for slot in slots], axis=1)
+        for piece in range(PIECES):
+            some = range(piece * bases // PIECES, (piece + 1) * bases // PIECES)
+            built = [jnp.concatenate([tiles[slot * bases + b] for slot in slots], axis=1) for b in some]
+            sums = nt(values, jnp.concatenate(built, axis=0))
+            for at, b in enumerate(some):
+                term = sums[:, at * rows : (at + 1) * rows] * weights[b]
+                total = term if total is None else total + term
+            for step in steps[piece * len(steps) // PIECES : (piece + 1) * len(steps) // PIECES]:
+                step()
         return total
+
+    def owed(value, slots):
+        for slot in slots:
+            built = tiles[pl.ds(slot * bases, bases)]
+            some = jnp.concatenate([built[b] for b in range(bases)], axis=1)
+            sums = jnp.dot(value, some, preferred_element_type=F32)
+            total = None
+            for b in range(bases):
+                term = sums[:, b * rows : (b + 1) * rows] * weights[b]
+                total = term if total is None else total + term
+            owes[slot] = total.astype(BF16)
+
+    def build_all(slot):
+        for step in build(slot):
+            step()
 
     fetched_pair(3)
     projected = nt(proj_ref[...], feat_ref[...])
@@ -271,8 +305,10 @@
     def _():
         with jax.named_scope("barrier"):
             pl.semaphore_wait(barrier, heard)
-        spread(0, (2, 1, 8, 6, 7, 3, 5, 4))
-        spread(1, (2, 1, 8, 6, 7, 3, 5, 4))
+        spread(0, (2, 1, 8, 6, 7))
+        spread(1, (2, 1, 8, 6, 7))
+        spread(0, (5, 3, 4))
+        spread(1, (5, 3, 4))
 
     with jax.named_scope("own"):
         columns = jnp.concatenate([place, jnp.zeros((5, rows), F32)], axis=0).T
@@ -283,7 +319,7 @@
         for b in range(bases):
             weights[b] = jnp.broadcast_to(radial[:, b : b + 1], (radial.shape[0], rows))
         fetched_pair(5)
-        build(0)
+        build_all(0)
         grad_act = nt(outw_ref[...], cot_ref[...])
 
     with jax.named_scope("spread"):
@@ -292,8 +328,8 @@
         def _():
             with jax.named_scope("barrier"):
                 pl.semaphore_wait(barrier, heard)
+            remote(packet_out.at[6:9], relay, send_sem.at[0], relay_sem, device(3)).start()
             spread(1, (3,))
-            remote(packet_out.at[6:9], relay, send_sem.at[0], relay_sem, device(3)).start()
             spread(0, (3,))
 
             @pl.when(odd_x)
@@ -318,16 +354,21 @@
                 pl.semaphore_wait(barrier, heard)
             pl.semaphore_signal(told_sem.at[1], inc=1, device_id=device(3), device_id_type=MESH)
             spread(0, (2, 1, 3, 5, 4))
-            spread(1, (2, 1, 3, 5, 4))
+            spread(1, (2, 3, 5, 4, 1))
+
+            def pass_on(kind, sources):
+                for column in (OUTER, SAME, INNER):
+                    there = 3 + column
+                    land = recv_sem.at[lands(kind, there)]
+                    to = (at_x[column], size_z - 1)
+                    remote(sources[column], held_at(kind, there), send_sem.at[kind], land, to).start()
+
             with jax.named_scope("relay"):
+                remote(relay, relay, send_sem.at[0], relay_sem, device(1)).wait_recv()
+            pass_on(0, [relay.at[column] for column in range(3)])
+            with jax.named_scope("relay1"):
                 arrived(1, 3, 4)
-                remote(relay, relay, send_sem.at[0], relay_sem, device(1)).wait_recv()
-            for column in (OUTER, SAME, INNER):
-                to = (at_x[column], size_z - 1)
-                there = 6 + column
-                for kind, src in ((0, relay.at[column]), (1, held_at(1, 3))):
-                    land = recv_sem.at[lands(kind, there)]
-                    remote(src, held_at(kind, there), send_sem.at[kind], land, to).start()
+            pass_on(1, [held_at(1, 3)] * 3)
             spread(0, (8, 6, 7))
             spread(1, (8, 6, 7))
 
@@ -341,36 +382,53 @@
             arrived(kind, low, slot + 1)
 
     message = None
-    for group in GROUPS:
-        for slot in group:
-            if slot:
-                with jax.named_scope(f"p{slot}"):
-                    take(0, slot)
-                with jax.named_scope("build"):
-                    build(slot)
-        with jax.named_scope(f"s{group[-1]}"):
-            for slot in WAITS[group]:
+    for at, (packets, features, group) in enumerate(STAGES):
+        with jax.named_scope(f"p{at}"):
+            for slot in packets:
+                take(0, slot)
+        with jax.named_scope(f"s{at}"):
+            for slot in features:
                 take(1, slot)
-        with jax.named_scope("gather"):
-            message = gathered(source, group, message)
+        with jax.named_scope("stage"):
+            if group:
+                message = gathered(group, message, packets)
+            else:
+                for slot in packets:
+                    build_all(slot)
 
     message = message * valid_row
-    gate = 1.0 / (1.0 + jnp.exp(-message))
+    gate = 0.5 + 0.5 * jnp.tanh(0.5 * message)
     grad_msg = grad_act * gate * (1.0 + message * (1.0 - gate)) * valid_row
-    grads[0] = grad_msg.astype(BF16)
-    with jax.named_scope("spread2"):
-        spread(2, (8, 6, 7, 3, 5, 4, 2, 1))
+    grad_msg = grad_msg.astype(BF16)
+    for turn in range(3):
+        level = jnp.where(first_z, turn, jnp.where(last_z, (1, 2, 0)[turn], (1, 0, 2)[turn]))
+        to_z = jnp.where(level == SOONER, at_z[SOONER], jnp.where(level == LATER, at_z[LATER], here_z))
+        there_z = jnp.where(level == SOONER, into_z[SOONER], jnp.where(level == LATER, into_z[LATER], 0))
+        land = recv_sem.at[15 + there_z // 3]
+        with jax.named_scope(f"owed{turn}"):
+            for columns in ((OUTER,), (SAME, INNER)) if turn == 0 else ((OUTER, SAME, INNER),):
+                owed(grad_msg, [3 * level + column for column in columns])
+                for column in columns:
+
+                    def send(column=column):
+                        src, dst = owes.at[3 * level + column], grads.at[there_z + column]
+                        remote(src, dst, send_sem.at[2], land, (at_x[column], to_z)).start()
+
+                    if column == SAME:
+                        pl.when(level != LEVEL)(send)
+                    else:
+                        send()
 
     activated = (message * gate).astype(BF16)
     both_ref[0] = (feat_ref[...].astype(F32) + tn(activated, outw_ref[...])).astype(BF16)
 
-    total = None
-    for group in GROUPS:
-        with jax.named_scope(f"g{group[-1]}"):
-            for slot in WAITS[group]:
-                take(2, slot)
-        with jax.named_scope("gather2"):
-            total = gathered(grads, group, total)
+    total = owes[0].astype(F32)
+    for low, high in ((1, 3), (3, 6), (6, 9)):
+        with jax.named_scope(f"g{high - 1}"):
+            held = grads.at[low:high]
+            remote(held, held, send_sem.at[2], recv_sem.at[15 + low // 3], device(1)).wait_recv()
+        for slot in range(low, high):
+            total += grads[slot].astype(F32)
     grad_proj = (total * valid_row).astype(BF16)
     pulled = tn(grad_proj, proj_ref[...])
     both_ref[1] = (cot_ref[...].astype(F32) + pulled).astype(BF16)
@@ -424,6 +482,7 @@
             pltpu.VMEM((bases, width, rows), F32),
             pltpu.VMEM((9, width, rows), BF16),
             pltpu.VMEM((9, width, rows), BF16),
+            pltpu.VMEM((9, width, rows), BF16),
             pltpu.SemaphoreType.DMA((6,)),
             pltpu.SemaphoreType.DMA,
             pltpu.SemaphoreType.REGULAR((2,)),

time: 17.8 us -> 17 us (0.955)
  Pallas kernels: 16.3 us -> 15.5 us
    pallas_call x1, Pallas kernels: 16.3 us -> 15.5 us  [on_device(): pl.pallas_call(functools.partial(kernel, atoms, bases), out_shape=pltpu.V...]
where the time goes in v2:
time: 17 us; the launch traced here: 16.8 us
  Pallas kernels  15.5 us (91%)
  between operations  0.64 us (4%)
  local copies, waits for them, and re-layouts  0.63 us (4%)
    pallas_call x1, Pallas kernels, on_device(): pl.pallas_call(functools.partial(kernel, atoms, bases), out_shape=pltpu.V...  15.5 us
    slice x1, local copies, waits for them, and re-layouts, on_device(): return (both[0].reshape(shape), both[1].reshape(shape))  0.63 us

profile of v2, /device:TPU:0, one launch (start us, length us, event | category | flops | bytes accessed | tf_op | source)
XLA Modules:
  0.0 16.8 jit_solution(11649878670506668320)
XLA Ops:
  0.6 15.5 %shard_map.95 = bf16[2,128,128]{2,1,0:T(8,128)(2,1)S(1)} custom-call(bf16[128,128]{1,0:T(8,128)(2,1)} %bitcast.12, bf16[128,128]{1,0:T(8,128)(2,1)} %bitcast.13, f32[6,1,64]{2,1,0:T(1,128)} %bitcast.17, s32[2]{0:T(128)} %bitcast.19, s32[2,27]{1,0:T(2,128)} %bitcast.18, bf16[64,128]{1,0:T(8,128)(2,1)} %bitcast.16, bf16[64,128]{1,0:T(8,128)(2,1)} %outw_hbm.1, ...), custom_call_target="tpu_custom_call" | custom-call | tf_op jit(solution)/shard_map/pallas_call | solution.py:470
  16.2 0.6 %fusion = (bf16[1,128,128]{2,1,0:T(8,128)(2,1)}, bf16[1,128,128]{2,1,0:T(8,128)(2,1)}) fusion(bf16[2,128,128]{2,1,0:T(8,128)(2,1)S(1)} %shard_map.95), kind=kLoop, calls=%fused_computation | loop fusion | bytes 131072 | tf_op jit(solution)/shard_map/slice | solution.py:494

commit v3 on v2

--- a/solution.py
+++ b/solution.py
@@ -21,11 +21,11 @@
 SLOTS.update({6 + at: (at, LATER) for at in (SAME, INNER, OUTER)})
 STAGES = (
     ((1,), (), ()),
-    ((2, 6), (1,), (0, 1)),
-    ((7, 8), (2, 6), (2, 6)),
-    ((), (7, 8), (7, 8)),
-    ((3,), (), ()),
-    ((5,), (), ()),
+    ((2,), (1,), (0, 1)),
+    ((6, 7), (2,), (2,)),
+    ((8,), (), ()),
+    ((3,), (6, 7), (6, 7)),
+    ((5,), (8,), (8,)),
     ((4,), (3, 5), (3, 5)),
     ((), (4,), (4,)),
 )
@@ -94,7 +94,7 @@
     off_x = (0, inward, -inward)
 
     def sooner_of(z):
-        return jnp.where(jnp.logical_or(z == 0, z == size_z - 1), 1, -1)
+        return jnp.where(z == size_z - 1, 1, -1)
 
     off_z = (0, sooner_of(here_z), -sooner_of(here_z))
     at_x = [here_x] + [lax.rem(here_x + off + size_x, size_x) for off in off_x[1:]]
@@ -175,7 +175,9 @@
             )
             for oy in (-1, 0, 1)
         ]
-        return jnp.concatenate([place] + listed + [jnp.zeros((2, rows), F32)], axis=0)
+        at = lax.rem(lane, atoms)
+        row = jnp.where(at == 0, listed[0], jnp.where(at == 1, listed[1], listed[2]))
+        return jnp.concatenate([place, row], axis=0)
 
     packet_in[0] = packet_for(0, 0)
     for slot, (column, level) in SLOTS.items():
@@ -197,7 +199,7 @@
     def lands(kind, slot):
         if kind == 0:
             return slot - 1
-        return 8 + (0, 1, 2, 3, 4, 5, 6, 6)[slot - 1]
+        return 8 + (0, 1, 2, 3, 4, 5, 5, 6)[slot - 1]
 
     def landing(kind, slot):
         level = SLOTS[slot][1]
@@ -211,15 +213,15 @@
             column, level = SLOTS[slot]
             src = packet_out.at[slot] if kind == 0 else held_at(kind, 0)
             there = slot_there(slot)
-            remote(src, held_at(kind, there), send_sem.at[kind], landing(kind, slot), device(slot)).start()
+            remote(src, held_at(kind, there), send_sem, landing(kind, slot), device(slot)).start()
 
     def arrived(kind, low, high):
         held = (packet_in, source, grads)[kind].at[low:high]
-        remote(held, held, send_sem.at[kind], recv_sem.at[lands(kind, low)], device(1)).wait_recv()
+        remote(held, held, send_sem, recv_sem.at[lands(kind, low)], device(1)).wait_recv()
 
     def sent(kind, count):
         some = (packet_in, source, grads)[kind].at[0:count]
-        remote(some, some, send_sem.at[kind], recv_sem.at[0], device(1)).wait_send()
+        remote(some, some, send_sem, recv_sem.at[0], device(1)).wait_send()
 
     def build(slot):
         column, level = SLOTS[slot] if slot else (SAME, LEVEL)
@@ -228,6 +230,9 @@
         other_x = packet[0:1] + 2.0 * (ox if column == SAME else ox.astype(F32))
         other_y = packet[1:2]
         other_z = packet[2:3] + 2.0 * (oz if level == LEVEL else oz.astype(F32))
+        theirs = [
+            jnp.where(upper, packet[3:4, atoms + at : atoms + at + 1], packet[3:4, at : at + 1]) for at in range(3)
+        ]
         chunk = 32
         half = bases // 2
 
@@ -258,7 +263,7 @@
         for c in range(2):
             cross = upper if c == 0 else jnp.logical_not(upper)
             low, same, high = (
-                packet[4 + oy : 5 + oy] * mask_ref[c, direction(ox, oy, oz)].astype(F32) for oy in (-1, 0, 1)
+                theirs[1 + oy] * mask_ref[c, direction(ox, oy, oz)].astype(F32) for oy in (-1, 0, 1)
             )
             gate_low = jnp.where(cross, low, same)
             gate_high = jnp.where(cross, high, same)
@@ -328,9 +333,9 @@
         def _():
             with jax.named_scope("barrier"):
                 pl.semaphore_wait(barrier, heard)
-            remote(packet_out.at[6:9], relay, send_sem.at[0], relay_sem, device(3)).start()
-            spread(1, (3,))
-            spread(0, (3,))
+            remote(packet_out.at[3:6], relay, send_sem, relay_sem, device(6)).start()
+            spread(1, (6,))
+            spread(0, (6,))
 
             @pl.when(odd_x)
             def _():
@@ -345,8 +350,8 @@
             spread(1, (2, 1))
             with jax.named_scope("told"):
                 pl.semaphore_wait(told_sem.at[1], 1)
-            spread(0, (5, 4))
-            spread(1, (5, 4))
+            spread(0, (8, 7))
+            spread(1, (8, 7))
 
         @pl.when(second_z)
         def _():
@@ -361,10 +366,10 @@
                     there = 3 + column
                     land = recv_sem.at[lands(kind, there)]
                     to = (at_x[column], size_z - 1)
-                    remote(sources[column], held_at(kind, there), send_sem.at[kind], land, to).start()
+                    remote(sources[column], held_at(kind, there), send_sem, land, to).start()
 
             with jax.named_scope("relay"):
-                remote(relay, relay, send_sem.at[0], relay_sem, device(1)).wait_recv()
+                remote(relay, relay, send_sem, relay_sem, device(1)).wait_recv()
             pass_on(0, [relay.at[column] for column in range(3)])
             with jax.named_scope("relay1"):
                 arrived(1, 3, 4)
@@ -401,7 +406,7 @@
     grad_msg = grad_act * gate * (1.0 + message * (1.0 - gate)) * valid_row
     grad_msg = grad_msg.astype(BF16)
     for turn in range(3):
-        level = jnp.where(first_z, turn, jnp.where(last_z, (1, 2, 0)[turn], (1, 0, 2)[turn]))
+        level = jnp.where(first_z, (0, 2, 1)[turn], jnp.where(last_z, (1, 2, 0)[turn], (1, 0, 2)[turn]))
         to_z = jnp.where(level == SOONER, at_z[SOONER], jnp.where(level == LATER, at_z[LATER], here_z))
         there_z = jnp.where(level == SOONER, into_z[SOONER], jnp.where(level == LATER, into_z[LATER], 0))
         land = recv_sem.at[15 + there_z // 3]
@@ -412,7 +417,7 @@
 
                     def send(column=column):
                         src, dst = owes.at[3 * level + column], grads.at[there_z + column]
-                        remote(src, dst, send_sem.at[2], land, (at_x[column], to_z)).start()
+                        remote(src, dst, send_sem, land, (at_x[column], to_z)).start()
 
                     if column == SAME:
                         pl.when(level != LEVEL)(send)
@@ -426,7 +431,7 @@
     for low, high in ((1, 3), (3, 6), (6, 9)):
         with jax.named_scope(f"g{high - 1}"):
             held = grads.at[low:high]
-            remote(held, held, send_sem.at[2], recv_sem.at[15 + low // 3], device(1)).wait_recv()
+            remote(held, held, send_sem, recv_sem.at[15 + low // 3], device(1)).wait_recv()
         for slot in range(low, high):
             total += grads[slot].astype(F32)
     grad_proj = (total * valid_row).astype(BF16)
@@ -474,9 +479,9 @@
         out_specs=pl.BlockSpec(memory_space=pltpu.VMEM),
         scratch_shapes=[space(x.shape, x.dtype) for space, x in zip(held, operands)]
         + [
-            pltpu.VMEM((9, 8, rows), F32),
-            pltpu.VMEM((9, 8, rows), F32),
-            pltpu.VMEM((3, 8, rows), F32),
+            pltpu.VMEM((9, 4, rows), F32),
+            pltpu.VMEM((9, 4, rows), F32),
+            pltpu.VMEM((3, 4, rows), F32),
             pltpu.VMEM((3, rows, rows), F32),
             pltpu.VMEM((9 * bases, rows, rows), BF16),
             pltpu.VMEM((bases, width, rows), F32),
@@ -486,7 +491,7 @@
             pltpu.SemaphoreType.DMA((6,)),
             pltpu.SemaphoreType.DMA,
             pltpu.SemaphoreType.REGULAR((2,)),
-            pltpu.SemaphoreType.DMA((3,)),
+            pltpu.SemaphoreType.DMA,
             pltpu.SemaphoreType.DMA((18,)),
         ],
         compiler_params=pltpu.CompilerParams(collective_id=0, has_side_effects=True),

time: 17 us -> 16.7 us (0.982)
  Pallas kernels: 15.5 us -> 15.2 us
    pallas_call x1, Pallas kernels: 15.5 us -> 15.2 us  [on_device(): pl.pallas_call(functools.partial(kernel, atoms, bases), out_shape=pltpu.V...]
where the time goes in v3:
time: 16.7 us; the launch traced here: 16.5 us
  Pallas kernels  15.2 us (91%)
  between operations  0.64 us (4%)
  local copies, waits for them, and re-layouts  0.63 us (4%)
    pallas_call x1, Pallas kernels, on_device(): pl.pallas_call(functools.partial(kernel, atoms, bases), out_shape=pltpu.V...  15.2 us
    slice x1, local copies, waits for them, and re-layouts, on_device(): return (both[0].reshape(shape), both[1].reshape(shape))  0.63 us

profile of v3, /device:TPU:0, one launch (start us, length us, event | category | flops | bytes accessed | tf_op | source)
XLA Modules:
  0.0 16.5 jit_solution(11925911154906977060)
XLA Ops:
  0.6 15.2 %shard_map.95 = bf16[2,128,128]{2,1,0:T(8,128)(2,1)S(1)} custom-call(bf16[128,128]{1,0:T(8,128)(2,1)} %bitcast.12, bf16[128,128]{1,0:T(8,128)(2,1)} %bitcast.13, f32[6,1,64]{2,1,0:T(1,128)} %bitcast.17, s32[2]{0:T(128)} %bitcast.19, s32[2,27]{1,0:T(2,128)} %bitcast.18, bf16[64,128]{1,0:T(8,128)(2,1)} %bitcast.16, bf16[64,128]{1,0:T(8,128)(2,1)} %outw_hbm.1, ...), custom_call_target="tpu_custom_call" | custom-call | tf_op jit(solution)/shard_map/pallas_call | solution.py:475
  15.9 0.6 %fusion = (bf16[1,128,128]{2,1,0:T(8,128)(2,1)}, bf16[1,128,128]{2,1,0:T(8,128)(2,1)}) fusion(bf16[2,128,128]{2,1,0:T(8,128)(2,1)S(1)} %shard_map.95), kind=kLoop, calls=%fused_computation | loop fusion | bytes 131072 | tf_op jit(solution)/shard_map/slice | solution.py:499

commit v4 on v3

--- a/solution.py
+++ b/solution.py
@@ -12,6 +12,7 @@
 F32 = jnp.float32
 BF16 = jnp.bfloat16
 LOG2E = 1.4426950408889634
+FALL = 2.718281828459045**-4
 PIECES = 4
 
 SAME, INNER, OUTER = 0, 1, 2
@@ -25,9 +26,10 @@
     ((6, 7), (2,), (2,)),
     ((8,), (), ()),
     ((3,), (6, 7), (6, 7)),
-    ((5,), (8,), (8,)),
-    ((4,), (3, 5), (3, 5)),
-    ((), (4,), (4,)),
+    ((), (3, 8), (3, 8)),
+    ((4,), (), ()),
+    ((5,), (), ()),
+    ((), (4, 5), (4, 5)),
 )
 
 
@@ -41,11 +43,6 @@
 
 def direction(ox, oy, oz):
     return (ox + 1) * 9 + (oy + 1) * 3 + oz + 1
-
-
-def basis_scale(bases):
-    off = lax.broadcasted_iota(jnp.int32, (bases, 1), 0).astype(F32) - 0.5 * (bases - 1)
-    return jnp.exp(-2.0 * off * off)
 
 
 def kernel(
@@ -198,8 +195,8 @@
 
     def lands(kind, slot):
         if kind == 0:
-            return slot - 1
-        return 8 + (0, 1, 2, 3, 4, 5, 5, 6)[slot - 1]
+            return (0, 1, 2, 3, 4, 5, 5, 6)[slot - 1]
+        return 7 + (0, 1, 2, 3, 3, 4, 4, 5)[slot - 1]
 
     def landing(kind, slot):
         level = SLOTS[slot][1]
@@ -252,10 +249,11 @@
                 envelope = jnp.where(at_row == at_lane, 0.0, envelope)
             rise = (4.0 * LOG2E * bases) * near - (4.0 * LOG2E * half)
             up, down = jnp.exp2(rise), jnp.exp2(-rise)
-            high = envelope * jnp.exp2(rise * (0.5 - rise * (0.125 / LOG2E)))
+            high = envelope * jnp.exp2(rise * (0.5 - rise * (0.125 / LOG2E)) - 0.5 * LOG2E)
             low = high * down
             for step_out in range(half):
                 if step_out:
+                    up, down = up * FALL, down * FALL
                     high, low = high * up, low * down
                 for b, value in ((half + step_out, high), (half - 1 - step_out, low)):
                     tiles[slot * bases + b, some, :] = value.astype(BF16)
@@ -320,7 +318,7 @@
         for axis in range(3):
             own_cols[axis] = jnp.broadcast_to(columns[:, axis : axis + 1], (rows, rows))
         fetches[5].wait()
-        radial = (radial_ref[...] * basis_scale(bases)).T
+        radial = radial_ref[...].T
         for b in range(bases):
             weights[b] = jnp.broadcast_to(radial[:, b : b + 1], (radial.shape[0], rows))
         fetched_pair(5)
@@ -359,7 +357,6 @@
                 pl.semaphore_wait(barrier, heard)
             pl.semaphore_signal(told_sem.at[1], inc=1, device_id=device(3), device_id_type=MESH)
             spread(0, (2, 1, 3, 5, 4))
-            spread(1, (2, 3, 5, 4, 1))
 
             def pass_on(kind, sources):
                 for column in (OUTER, SAME, INNER):
@@ -374,13 +371,12 @@
             with jax.named_scope("relay1"):
                 arrived(1, 3, 4)
             pass_on(1, [held_at(1, 3)] * 3)
+            spread(1, (2, 3, 5, 4, 1))
             spread(0, (8, 6, 7))
             spread(1, (8, 6, 7))
 
     def take(kind, slot):
-        if kind == 0:
-            arrived(0, slot, slot + 1)
-        elif kind == 1 and slot == 3:
+        if kind == 1 and slot == 3:
             pl.when(jnp.logical_not(second_z))(lambda: arrived(1, 3, 4))
         elif slot == 8 or lands(kind, slot + 1) != lands(kind, slot):
             low = min(at for at in range(1, 9) if lands(kind, at) == lands(kind, slot))
@@ -406,10 +402,10 @@
     grad_msg = grad_act * gate * (1.0 + message * (1.0 - gate)) * valid_row
     grad_msg = grad_msg.astype(BF16)
     for turn in range(3):
-        level = jnp.where(first_z, (0, 2, 1)[turn], jnp.where(last_z, (1, 2, 0)[turn], (1, 0, 2)[turn]))
+        level = jnp.where(last_z, (1, 2, 0)[turn], jnp.where(second_z, (1, 0, 2)[turn], (0, 2, 1)[turn]))
         to_z = jnp.where(level == SOONER, at_z[SOONER], jnp.where(level == LATER, at_z[LATER], here_z))
         there_z = jnp.where(level == SOONER, into_z[SOONER], jnp.where(level == LATER, into_z[LATER], 0))
-        land = recv_sem.at[15 + there_z // 3]
+        land = recv_sem.at[13 + there_z // 3]
         with jax.named_scope(f"owed{turn}"):
             for columns in ((OUTER,), (SAME, INNER)) if turn == 0 else ((OUTER, SAME, INNER),):
                 owed(grad_msg, [3 * level + column for column in columns])
@@ -431,7 +427,7 @@
     for low, high in ((1, 3), (3, 6), (6, 9)):
         with jax.named_scope(f"g{high - 1}"):
             held = grads.at[low:high]
-            remote(held, held, send_sem, recv_sem.at[15 + low // 3], device(1)).wait_recv()
+            remote(held, held, send_sem, recv_sem.at[13 + low // 3], device(1)).wait_recv()
         for slot in range(low, high):
             total += grads[slot].astype(F32)
     grad_proj = (total * valid_row).astype(BF16)
@@ -492,7 +488,7 @@
             pltpu.SemaphoreType.DMA,
             pltpu.SemaphoreType.REGULAR((2,)),
             pltpu.SemaphoreType.DMA,
-            pltpu.SemaphoreType.DMA((18,)),
+            pltpu.SemaphoreType.DMA((16,)),
         ],
         compiler_params=pltpu.CompilerParams(collective_id=0, has_side_effects=True),
     )(*operands)

time: 16.7 us -> 16.7 us (level)
  no operation moved by 1% of the time
where the time goes in v4:
time: 16.7 us; the launch traced here: 16.5 us
  Pallas kernels  15.2 us (91%)
  between operations  0.64 us (4%)
  local copies, waits for them, and re-layouts  0.63 us (4%)
    pallas_call x1, Pallas kernels, on_device(): pl.pallas_call(functools.partial(kernel, atoms, bases), out_shape=pltpu.V...  15.2 us
    slice x1, local copies, waits for them, and re-layouts, on_device(): return (both[0].reshape(shape), both[1].reshape(shape))  0.63 us

profile of v4, /device:TPU:0, one launch (start us, length us, event | category | flops | bytes accessed | tf_op | source)
XLA Modules:
  0.0 16.5 jit_solution(2647429104366558733)
XLA Ops:
  0.6 15.2 %shard_map.95 = bf16[2,128,128]{2,1,0:T(8,128)(2,1)S(1)} custom-call(bf16[128,128]{1,0:T(8,128)(2,1)} %bitcast.12, bf16[128,128]{1,0:T(8,128)(2,1)} %bitcast.13, f32[6,1,64]{2,1,0:T(1,128)} %bitcast.17, s32[2]{0:T(128)} %bitcast.19, s32[2,27]{1,0:T(2,128)} %bitcast.18, bf16[64,128]{1,0:T(8,128)(2,1)} %bitcast.16, bf16[64,128]{1,0:T(8,128)(2,1)} %outw_hbm.1, ...), custom_call_target="tpu_custom_call" | custom-call | tf_op jit(solution)/shard_map/pallas_call | solution.py:471
  15.9 0.6 %fusion = (bf16[1,128,128]{2,1,0:T(8,128)(2,1)}, bf16[1,128,128]{2,1,0:T(8,128)(2,1)}) fusion(bf16[2,128,128]{2,1,0:T(8,128)(2,1)S(1)} %shard_map.95), kind=kLoop, calls=%fused_computation | loop fusion | bytes 131072 | tf_op jit(solution)/shard_map/slice | solution.py:495

commit v5 on v4

--- a/solution.py
+++ b/solution.py
@@ -230,7 +230,7 @@
         theirs = [
             jnp.where(upper, packet[3:4, atoms + at : atoms + at + 1], packet[3:4, at : at + 1]) for at in range(3)
         ]
-        chunk = 32
+        chunk = 16
         half = bases // 2
 
         def step(first, gate_low, gate_high, move):
@@ -402,7 +402,7 @@
     grad_msg = grad_act * gate * (1.0 + message * (1.0 - gate)) * valid_row
     grad_msg = grad_msg.astype(BF16)
     for turn in range(3):
-        level = jnp.where(last_z, (1, 2, 0)[turn], jnp.where(second_z, (1, 0, 2)[turn], (0, 2, 1)[turn]))
+        level = jnp.where(last_z, (1, 0, 2)[turn], jnp.where(second_z, (1, 0, 2)[turn], (0, 2, 1)[turn]))
         to_z = jnp.where(level == SOONER, at_z[SOONER], jnp.where(level == LATER, at_z[LATER], here_z))
         there_z = jnp.where(level == SOONER, into_z[SOONER], jnp.where(level == LATER, into_z[LATER], 0))
         land = recv_sem.at[13 + there_z // 3]

time: 16.7 us -> 16.7 us (level)
  no operation moved by 1% of the time
where the time goes in v5:
time: 16.7 us; the launch traced here: 16.5 us
  Pallas kernels  15.3 us (92%)
  between operations  0.64 us (4%)
  local copies, waits for them, and re-layouts  0.63 us (4%)
    pallas_call x1, Pallas kernels, on_device(): pl.pallas_call(functools.partial(kernel, atoms, bases), out_shape=pltpu.V...  15.3 us
    slice x1, local copies, waits for them, and re-layouts, on_device(): return (both[0].reshape(shape), both[1].reshape(shape))  0.63 us

profile of v5, /device:TPU:0, one launch (start us, length us, event | category | flops | bytes accessed | tf_op | source)
XLA Modules:
  0.0 16.5 jit_solution(7327141259140380137)
XLA Ops:
  0.6 15.3 %shard_map.95 = bf16[2,128,128]{2,1,0:T(8,128)(2,1)S(1)} custom-call(bf16[128,128]{1,0:T(8,128)(2,1)} %bitcast.12, bf16[128,128]{1,0:T(8,128)(2,1)} %bitcast.13, f32[6,1,64]{2,1,0:T(1,128)} %bitcast.17, s32[2]{0:T(128)} %bitcast.19, s32[2,27]{1,0:T(2,128)} %bitcast.18, bf16[64,128]{1,0:T(8,128)(2,1)} %bitcast.16, bf16[64,128]{1,0:T(8,128)(2,1)} %outw_hbm.1, ...), custom_call_target="tpu_custom_call" | custom-call | tf_op jit(solution)/shard_map/pallas_call | solution.py:471
  15.9 0.6 %fusion = (bf16[1,128,128]{2,1,0:T(8,128)(2,1)}, bf16[1,128,128]{2,1,0:T(8,128)(2,1)}) fusion(bf16[2,128,128]{2,1,0:T(8,128)(2,1)S(1)} %shard_map.95), kind=kLoop, calls=%fused_computation | loop fusion | bytes 131072 | tf_op jit(solution)/shard_map/slice | solution.py:495
